TPU v7x, 256 devices: a whole 4x4x8 slice. The times are simulated.
256 devices in a mesh: graph: 32 (over z, x_hi, core), feat: 8 (over x_lo, y).
Axes of the slice: x: 4 (x_hi: 2, x_lo: 2; x = x_hi * 2 + x_lo), y: 4, z: 8, core: 2. Of those that a mesh axis runs over, the one named last changes fastest.
Arguments:
- features: bfloat16 [256, 65536], P('feat', 'graph'), may hold values from -6 to 6
- tiles: bfloat16 [8192, 128, 128], P('graph'), may hold values from 0 to 0.049316406
- tile_source: int32 [8192], P('graph'), may hold values from 0 to 511, as said below
- tile_target: int32 [8192], P('graph'), may hold values from 0 to 15
- tile_count: int32 [32], P('graph'), may hold values from 88 to 256, as said below
- weight: bfloat16 [256, 256], replicated, may hold values from -0.375 to 0.375
Outputs:
- layer_output: bfloat16 [256, 65536], P('feat', 'graph')
Inputs may be any that keep to these rules, and one draw needn't show every extreme that they name: Within the 256 slots of each slab, the source slab tile_source // 16 never falls from one slot to the next. The used slots of a slab hold at least one tile from every slab's node blocks and at most 16 from any one slab's, and exactly 16 from some slab's, on every slab. `tile_count`: some slab uses all 256 slots.
All inputs are finite; a program needn't handle non-finite values.
Results may differ from a plain program's by a relative error of at most 0.0049.
Values may be sent and summed in bfloat16 or wider, within the bound.
No kernel may reach another device: no remote copies, remote signals or barrier semaphores. Data moves between devices by JAX's collectives and lax.ppermute only.
A program may use at most 64 MiB of HBM per device.

v0:
```python
import jax
import jax.numpy as jnp
from jax import lax
from jax.sharding import PartitionSpec as P

PAIR_MOST = 16


def shifted(block, axis, distance):
    devices = range(lax.axis_size(axis))
    route = [((i - distance) % len(devices), i) for i in devices]
    return lax.ppermute(block, axis, route)


def add_tiles(totals, visitor, tile_group, source_blocks, target_blocks, keep_mask):
    feature_rows = visitor.shape[0]
    tile_side = tile_group.shape[1]
    blocks = visitor.reshape(feature_rows, -1, tile_side)
    picked = jnp.take(blocks, source_blocks, axis=1)
    products = jnp.einsum("hwj,wij->hwi", picked, tile_group, preferred_element_type=jnp.float32)
    masked = products * keep_mask.astype(jnp.float32)[None, :, None]
    return totals.at[:, target_blocks, :].add(masked)


def body(features, tiles, tile_source, tile_target, tile_count, weight):
    slab_count = lax.axis_size("graph")
    position = lax.axis_index("graph")
    feature_rows, slab_nodes = features.shape
    tile_side = tiles.shape[1]
    block_count = slab_nodes // tile_side
    slot_total = tiles.shape[0]
    usable = jnp.arange(slot_total) < tile_count[0]
    source_slab = tile_source // block_count
    local_source = tile_source % block_count
    zero_totals = jnp.zeros((feature_rows, block_count, tile_side), jnp.float32)

    def add_slab(totals, visitor, slab_index):
        before = jnp.sum(((source_slab < slab_index) & usable).astype(jnp.int32))
        first_slot = jnp.minimum(before, slot_total - PAIR_MOST)
        window = lax.dynamic_slice_in_dim(tiles, first_slot, PAIR_MOST, 0)
        sources = lax.dynamic_slice_in_dim(local_source, first_slot, PAIR_MOST, 0)
        targets = lax.dynamic_slice_in_dim(tile_target, first_slot, PAIR_MOST, 0)
        keep_mask = lax.dynamic_slice_in_dim(
            (source_slab == slab_index) & usable, first_slot, PAIR_MOST, 0
        )
        return add_tiles(totals, visitor, window, sources, targets, keep_mask)

    def forward_turn(turn_index, running):
        totals, visitor = running
        visitor = shifted(visitor, "graph", 1)
        return (add_slab(totals, visitor, (position - turn_index) % slab_count), visitor)

    totals, last_visitor = lax.fori_loop(
        1, slab_count, forward_turn, (add_slab(zero_totals, features, position), features)
    )
    rounded = totals.reshape(feature_rows, slab_nodes).astype(jnp.bfloat16)
    columns = lax.dynamic_slice_in_dim(
        weight, lax.axis_index("feat") * feature_rows, feature_rows, 1
    )
    combined = jnp.einsum(
        "ko,kn->on",
        columns,
        lax.all_gather(rounded, "feat", axis=0, tiled=True),
        preferred_element_type=jnp.float32,
    )
    return jnp.maximum(combined, 0.0).astype(jnp.bfloat16)


def solution(mesh):
    return jax.shard_map(
        body,
        mesh=mesh,
        in_specs=(
            P("feat", "graph"),
            P("graph", None, None),
            P("graph"),
            P("graph"),
            P("graph"),
            P(),
        ),
        out_specs=P("feat", "graph"),
        check_vma=False,
    )
```

profile of v0, /device:TPU:4, one launch (start us, length us, event | category | flops | bytes accessed | tf_op | source)
XLA Modules:
  0.0 421.0 jit_solution(14925830925300414950)
XLA Ops:
  15.0 344.0 %while.18 = (s32[]{:T(128)}, f32[32,16,128]{2,0,1:T(8,128)S(1)}, bf16[32,2048]{1,0:T(8,128)(2,1)S(1)}, s32[]{:T(128)}, s32[256]{0:T(256)S(1)}, /*index=5*/s32[25...) while((s32[]{:T(128)}, f32[32,16,128]{2,0,1:T(8,128)S(1)}, ...), condition=%wide.region_5.7_spmd.clone, body=%wide.region_2.6_spmd.clone.sunk | while | flops 16977072 | bytes 3022064 | solution.py:53
  18.5 2.5 collective-permute-done
  21.6 1.5 fusion.35
  27.8 2.5 collective-permute-done
  30.9 1.5 fusion.35
  37.5 2.1 collective-permute-done
  40.2 1.5 fusion.35
  49.4 1.5 fusion.35
  52.2 2.3 collective-permute-start
  59.8 1.5 fusion.35
  62.5 2.1 collective-permute-start
  68.0 2.5 collective-permute-done
  71.2 1.5 fusion.35
  78.2 3.8 collective-permute-done
  82.6 1.5 fusion.35
  88.8 4.6 %collective-permute-done = bf16[32,2048]{1,0:T(8,128)(2,1)S(1)} collective-permute-done((bf16[32,2048]{1,0:T(8,128)(2,1)S(1)}, bf16[32,2048]{1,0:T(8,128)(2,1)S(1)}, u32[]{:S(2)}, u32[]{:S(2)}) %collective-permute-start) | collective-permute-done | bytes 131104 | tf_op jit(solution)/shard_map/while/body/eval_jaxpr/ppermute | solution.py:12
  94.0 1.5 fusion.35
  100.2 4.6 %collective-permute-done = bf16[32,2048]{1,0:T(8,128)(2,1)S(1)} collective-permute-done((bf16[32,2048]{1,0:T(8,128)(2,1)S(1)}, bf16[32,2048]{1,0:T(8,128)(2,1)S(1)}, u32[]{:S(2)}, u32[]{:S(2)}) %collective-permute-start) | collective-permute-done | bytes 131104 | tf_op jit(solution)/shard_map/while/body/eval_jaxpr/ppermute | solution.py:12
  105.4 1.5 fusion.35
  111.6 4.6 %collective-permute-done = bf16[32,2048]{1,0:T(8,128)(2,1)S(1)} collective-permute-done((bf16[32,2048]{1,0:T(8,128)(2,1)S(1)}, bf16[32,2048]{1,0:T(8,128)(2,1)S(1)}, u32[]{:S(2)}, u32[]{:S(2)}) %collective-permute-start) | collective-permute-done | bytes 131104 | tf_op jit(solution)/shard_map/while/body/eval_jaxpr/ppermute | solution.py:12
  116.8 1.5 fusion.35
  123.0 4.6 %collective-permute-done = bf16[32,2048]{1,0:T(8,128)(2,1)S(1)} collective-permute-done((bf16[32,2048]{1,0:T(8,128)(2,1)S(1)}, bf16[32,2048]{1,0:T(8,128)(2,1)S(1)}, u32[]{:S(2)}, u32[]{:S(2)}) %collective-permute-start) | collective-permute-done | bytes 131104 | tf_op jit(solution)/shard_map/while/body/eval_jaxpr/ppermute | solution.py:12
  128.2 1.5 fusion.35
  134.4 4.6 %collective-permute-done = bf16[32,2048]{1,0:T(8,128)(2,1)S(1)} collective-permute-done((bf16[32,2048]{1,0:T(8,128)(2,1)S(1)}, bf16[32,2048]{1,0:T(8,128)(2,1)S(1)}, u32[]{:S(2)}, u32[]{:S(2)}) %collective-permute-start) | collective-permute-done | bytes 131104 | tf_op jit(solution)/shard_map/while/body/eval_jaxpr/ppermute | solution.py:12
  139.6 1.5 fusion.35
  145.8 4.6 %collective-permute-done = bf16[32,2048]{1,0:T(8,128)(2,1)S(1)} collective-permute-done((bf16[32,2048]{1,0:T(8,128)(2,1)S(1)}, bf16[32,2048]{1,0:T(8,128)(2,1)S(1)}, u32[]{:S(2)}, u32[]{:S(2)}) %collective-permute-start) | collective-permute-done | bytes 131104 | tf_op jit(solution)/shard_map/while/body/eval_jaxpr/ppermute | solution.py:12
  151.0 1.5 fusion.35
  157.2 4.6 %collective-permute-done = bf16[32,2048]{1,0:T(8,128)(2,1)S(1)} collective-permute-done((bf16[32,2048]{1,0:T(8,128)(2,1)S(1)}, bf16[32,2048]{1,0:T(8,128)(2,1)S(1)}, u32[]{:S(2)}, u32[]{:S(2)}) %collective-permute-start) | collective-permute-done | bytes 131104 | tf_op jit(solution)/shard_map/while/body/eval_jaxpr/ppermute | solution.py:12
  162.4 1.5 fusion.35
  168.6 4.6 %collective-permute-done = bf16[32,2048]{1,0:T(8,128)(2,1)S(1)} collective-permute-done((bf16[32,2048]{1,0:T(8,128)(2,1)S(1)}, bf16[32,2048]{1,0:T(8,128)(2,1)S(1)}, u32[]{:S(2)}, u32[]{:S(2)}) %collective-permute-start) | collective-permute-done | bytes 131104 | tf_op jit(solution)/shard_map/while/body/eval_jaxpr/ppermute | solution.py:12
  173.8 1.5 fusion.35
  180.0 4.6 %collective-permute-done = bf16[32,2048]{1,0:T(8,128)(2,1)S(1)} collective-permute-done((bf16[32,2048]{1,0:T(8,128)(2,1)S(1)}, bf16[32,2048]{1,0:T(8,128)(2,1)S(1)}, u32[]{:S(2)}, u32[]{:S(2)}) %collective-permute-start) | collective-permute-done | bytes 131104 | tf_op jit(solution)/shard_map/while/body/eval_jaxpr/ppermute | solution.py:12
  185.2 1.5 fusion.35
  191.4 4.6 %collective-permute-done = bf16[32,2048]{1,0:T(8,128)(2,1)S(1)} collective-permute-done((bf16[32,2048]{1,0:T(8,128)(2,1)S(1)}, bf16[32,2048]{1,0:T(8,128)(2,1)S(1)}, u32[]{:S(2)}, u32[]{:S(2)}) %collective-permute-start) | collective-permute-done | bytes 131104 | tf_op jit(solution)/shard_map/while/body/eval_jaxpr/ppermute | solution.py:12
  196.6 1.5 fusion.35
  202.8 4.6 %collective-permute-done = bf16[32,2048]{1,0:T(8,128)(2,1)S(1)} collective-permute-done((bf16[32,2048]{1,0:T(8,128)(2,1)S(1)}, bf16[32,2048]{1,0:T(8,128)(2,1)S(1)}, u32[]{:S(2)}, u32[]{:S(2)}) %collective-permute-start) | collective-permute-done | bytes 131104 | tf_op jit(solution)/shard_map/while/body/eval_jaxpr/ppermute | solution.py:12
  208.0 1.5 fusion.35
  214.2 4.6 %collective-permute-done = bf16[32,2048]{1,0:T(8,128)(2,1)S(1)} collective-permute-done((bf16[32,2048]{1,0:T(8,128)(2,1)S(1)}, bf16[32,2048]{1,0:T(8,128)(2,1)S(1)}, u32[]{:S(2)}, u32[]{:S(2)}) %collective-permute-start) | collective-permute-done | bytes 131104 | tf_op jit(solution)/shard_map/while/body/eval_jaxpr/ppermute | solution.py:12
  219.4 1.5 fusion.35
  225.6 4.6 %collective-permute-done = bf16[32,2048]{1,0:T(8,128)(2,1)S(1)} collective-permute-done((bf16[32,2048]{1,0:T(8,128)(2,1)S(1)}, bf16[32,2048]{1,0:T(8,128)(2,1)S(1)}, u32[]{:S(2)}, u32[]{:S(2)}) %collective-permute-start) | collective-permute-done | bytes 131104 | tf_op jit(solution)/shard_map/while/body/eval_jaxpr/ppermute | solution.py:12
  230.8 1.5 fusion.35
  237.0 4.6 %collective-permute-done = bf16[32,2048]{1,0:T(8,128)(2,1)S(1)} collective-permute-done((bf16[32,2048]{1,0:T(8,128)(2,1)S(1)}, bf16[32,2048]{1,0:T(8,128)(2,1)S(1)}, u32[]{:S(2)}, u32[]{:S(2)}) %collective-permute-start) | collective-permute-done | bytes 131104 | tf_op jit(solution)/shard_map/while/body/eval_jaxpr/ppermute | solution.py:12
  242.2 1.5 fusion.35
  248.4 4.6 %collective-permute-done = bf16[32,2048]{1,0:T(8,128)(2,1)S(1)} collective-permute-done((bf16[32,2048]{1,0:T(8,128)(2,1)S(1)}, bf16[32,2048]{1,0:T(8,128)(2,1)S(1)}, u32[]{:S(2)}, u32[]{:S(2)}) %collective-permute-start) | collective-permute-done | bytes 131104 | tf_op jit(solution)/shard_map/while/body/eval_jaxpr/ppermute | solution.py:12
  253.6 1.5 fusion.35
  259.8 4.6 %collective-permute-done = bf16[32,2048]{1,0:T(8,128)(2,1)S(1)} collective-permute-done((bf16[32,2048]{1,0:T(8,128)(2,1)S(1)}, bf16[32,2048]{1,0:T(8,128)(2,1)S(1)}, u32[]{:S(2)}, u32[]{:S(2)}) %collective-permute-start) | collective-permute-done | bytes 131104 | tf_op jit(solution)/shard_map/while/body/eval_jaxpr/ppermute | solution.py:12
  265.0 1.5 fusion.35
  271.2 4.6 %collective-permute-done = bf16[32,2048]{1,0:T(8,128)(2,1)S(1)} collective-permute-done((bf16[32,2048]{1,0:T(8,128)(2,1)S(1)}, bf16[32,2048]{1,0:T(8,128)(2,1)S(1)}, u32[]{:S(2)}, u32[]{:S(2)}) %collective-permute-start) | collective-permute-done | bytes 131104 | tf_op jit(solution)/shard_map/while/body/eval_jaxpr/ppermute | solution.py:12
  276.4 1.5 fusion.35
  282.6 4.6 %collective-permute-done = bf16[32,2048]{1,0:T(8,128)(2,1)S(1)} collective-permute-done((bf16[32,2048]{1,0:T(8,128)(2,1)S(1)}, bf16[32,2048]{1,0:T(8,128)(2,1)S(1)}, u32[]{:S(2)}, u32[]{:S(2)}) %collective-permute-start) | collective-permute-done | bytes 131104 | tf_op jit(solution)/shard_map/while/body/eval_jaxpr/ppermute | solution.py:12
  287.8 1.5 fusion.35
  294.0 4.6 %collective-permute-done = bf16[32,2048]{1,0:T(8,128)(2,1)S(1)} collective-permute-done((bf16[32,2048]{1,0:T(8,128)(2,1)S(1)}, bf16[32,2048]{1,0:T(8,128)(2,1)S(1)}, u32[]{:S(2)}, u32[]{:S(2)}) %collective-permute-start) | collective-permute-done | bytes 131104 | tf_op jit(solution)/shard_map/while/body/eval_jaxpr/ppermute | solution.py:12
  299.2 1.5 fusion.35
  305.5 4.6 %collective-permute-done = bf16[32,2048]{1,0:T(8,128)(2,1)S(1)} collective-permute-done((bf16[32,2048]{1,0:T(8,128)(2,1)S(1)}, bf16[32,2048]{1,0:T(8,128)(2,1)S(1)}, u32[]{:S(2)}, u32[]{:S(2)}) %collective-permute-start) | collective-permute-done | bytes 131104 | tf_op jit(solution)/shard_map/while/body/eval_jaxpr/ppermute | solution.py:12
  310.6 1.5 fusion.35
  316.9 4.6 %collective-permute-done = bf16[32,2048]{1,0:T(8,128)(2,1)S(1)} collective-permute-done((bf16[32,2048]{1,0:T(8,128)(2,1)S(1)}, bf16[32,2048]{1,0:T(8,128)(2,1)S(1)}, u32[]{:S(2)}, u32[]{:S(2)}) %collective-permute-start) | collective-permute-done | bytes 131104 | tf_op jit(solution)/shard_map/while/body/eval_jaxpr/ppermute | solution.py:12
  322.0 1.5 fusion.35
  328.3 4.6 %collective-permute-done = bf16[32,2048]{1,0:T(8,128)(2,1)S(1)} collective-permute-done((bf16[32,2048]{1,0:T(8,128)(2,1)S(1)}, bf16[32,2048]{1,0:T(8,128)(2,1)S(1)}, u32[]{:S(2)}, u32[]{:S(2)}) %collective-permute-start) | collective-permute-done | bytes 131104 | tf_op jit(solution)/shard_map/while/body/eval_jaxpr/ppermute | solution.py:12
  333.4 1.5 fusion.35
  339.7 4.6 %collective-permute-done = bf16[32,2048]{1,0:T(8,128)(2,1)S(1)} collective-permute-done((bf16[32,2048]{1,0:T(8,128)(2,1)S(1)}, bf16[32,2048]{1,0:T(8,128)(2,1)S(1)}, u32[]{:S(2)}, u32[]{:S(2)}) %collective-permute-start) | collective-permute-done | bytes 131104 | tf_op jit(solution)/shard_map/while/body/eval_jaxpr/ppermute | solution.py:12
  344.8 1.5 fusion.35
  351.1 4.6 %collective-permute-done = bf16[32,2048]{1,0:T(8,128)(2,1)S(1)} collective-permute-done((bf16[32,2048]{1,0:T(8,128)(2,1)S(1)}, bf16[32,2048]{1,0:T(8,128)(2,1)S(1)}, u32[]{:S(2)}, u32[]{:S(2)}) %collective-permute-start) | collective-permute-done | bytes 131104 | tf_op jit(solution)/shard_map/while/body/eval_jaxpr/ppermute | solution.py:12
  359.7 52.2 %all-gather.2.cloned.1.call-done = bf16[256,2048]{1,0:T(8,128)(2,1)} async-done(((bf16[32,2048]{1,0:T(8,128)(2,1)}), bf16[256,2048]{1,0:T(8,128)(2,1)}) %all-gather.2.cloned.1.call-update) | async-done | bytes 1048592 | tf_op jit(solution)/shard_map/all_gather | solution.py:63
  411.9 2.3 fusion.11
  (359 shorter events, 161.1 us)
Async XLA Ops:
  6.5 405.3 %copy-start = (bf16[256,256]{1,0:T(8,128)(2,1)S(1)}, bf16[256,256]{1,0:T(8,128)(2,1)}, u32[]{:S(2)}) copy-start(bf16[256,256]{1,0:T(8,128)(2,1)} %param.15) | copy-start | bytes 393220
  6.5 405.3 %all-gather.2.cloned.1.call-start = ((), (), s32[]{:S(2)}) async-start(), calls=%async_computation | async-start | bytes 1179648 | tf_op jit(solution)/shard_map/all_gather | solution.py:63
  15.0 6.0 %collective-permute-start = (bf16[32,2048]{1,0:T(8,128)(2,1)S(1)}, bf16[32,2048]{1,0:T(8,128)(2,1)S(1)}, u32[]{:S(2)}, u32[]{:S(2)}) collective-permute-start(bf16[32,2048]{1,0:T(8,128)(2,1)S(1)} %get-tuple-element.350), channel_id=1, source_target_pairs={{248,0},{0,8},{8,16},{16,24},{24,32},{32,40},{40,48},{48,56},{56,6... | collective-permute-start | bytes 393224 | tf_op jit(solution)/shard_map/while/body/eval_jaxpr/ppermute | solution.py:12
  24.3 6.0 %collective-permute-start = (bf16[32,2048]{1,0:T(8,128)(2,1)S(1)}, bf16[32,2048]{1,0:T(8,128)(2,1)S(1)}, u32[]{:S(2)}, u32[]{:S(2)}) collective-permute-start(bf16[32,2048]{1,0:T(8,128)(2,1)S(1)} %get-tuple-element.350), channel_id=1, source_target_pairs={{248,0},{0,8},{8,16},{16,24},{24,32},{32,40},{40,48},{48,56},{56,6... | collective-permute-start | bytes 393224 | tf_op jit(solution)/shard_map/while/body/eval_jaxpr/ppermute | solution.py:12
  33.6 6.0 %collective-permute-start = (bf16[32,2048]{1,0:T(8,128)(2,1)S(1)}, bf16[32,2048]{1,0:T(8,128)(2,1)S(1)}, u32[]{:S(2)}, u32[]{:S(2)}) collective-permute-start(bf16[32,2048]{1,0:T(8,128)(2,1)S(1)} %get-tuple-element.350), channel_id=1, source_target_pairs={{248,0},{0,8},{8,16},{16,24},{24,32},{32,40},{40,48},{48,56},{56,6... | collective-permute-start | bytes 393224 | tf_op jit(solution)/shard_map/while/body/eval_jaxpr/ppermute | solution.py:12
  42.9 6.0 %collective-permute-start = (bf16[32,2048]{1,0:T(8,128)(2,1)S(1)}, bf16[32,2048]{1,0:T(8,128)(2,1)S(1)}, u32[]{:S(2)}, u32[]{:S(2)}) collective-permute-start(bf16[32,2048]{1,0:T(8,128)(2,1)S(1)} %get-tuple-element.350), channel_id=1, source_target_pairs={{248,0},{0,8},{8,16},{16,24},{24,32},{32,40},{40,48},{48,56},{56,6... | collective-permute-start | bytes 393224 | tf_op jit(solution)/shard_map/while/body/eval_jaxpr/ppermute | solution.py:12
  52.2 7.0 %collective-permute-start = (bf16[32,2048]{1,0:T(8,128)(2,1)S(1)}, bf16[32,2048]{1,0:T(8,128)(2,1)S(1)}, u32[]{:S(2)}, u32[]{:S(2)}) collective-permute-start(bf16[32,2048]{1,0:T(8,128)(2,1)S(1)} %get-tuple-element.350), channel_id=1, source_target_pairs={{248,0},{0,8},{8,16},{16,24},{24,32},{32,40},{40,48},{48,56},{56,6... | collective-permute-start | bytes 393224 | tf_op jit(solution)/shard_map/while/body/eval_jaxpr/ppermute | solution.py:12
  62.5 8.1 %collective-permute-start = (bf16[32,2048]{1,0:T(8,128)(2,1)S(1)}, bf16[32,2048]{1,0:T(8,128)(2,1)S(1)}, u32[]{:S(2)}, u32[]{:S(2)}) collective-permute-start(bf16[32,2048]{1,0:T(8,128)(2,1)S(1)} %get-tuple-element.350), channel_id=1, source_target_pairs={{248,0},{0,8},{8,16},{16,24},{24,32},{32,40},{40,48},{48,56},{56,6... | collective-permute-start | bytes 393224 | tf_op jit(solution)/shard_map/while/body/eval_jaxpr/ppermute | solution.py:12
  73.9 8.1 %collective-permute-start = (bf16[32,2048]{1,0:T(8,128)(2,1)S(1)}, bf16[32,2048]{1,0:T(8,128)(2,1)S(1)}, u32[]{:S(2)}, u32[]{:S(2)}) collective-permute-start(bf16[32,2048]{1,0:T(8,128)(2,1)S(1)} %get-tuple-element.350), channel_id=1, source_target_pairs={{248,0},{0,8},{8,16},{16,24},{24,32},{32,40},{40,48},{48,56},{56,6... | collective-permute-start | bytes 393224 | tf_op jit(solution)/shard_map/while/body/eval_jaxpr/ppermute | solution.py:12
  85.3 8.1 %collective-permute-start = (bf16[32,2048]{1,0:T(8,128)(2,1)S(1)}, bf16[32,2048]{1,0:T(8,128)(2,1)S(1)}, u32[]{:S(2)}, u32[]{:S(2)}) collective-permute-start(bf16[32,2048]{1,0:T(8,128)(2,1)S(1)} %get-tuple-element.350), channel_id=1, source_target_pairs={{248,0},{0,8},{8,16},{16,24},{24,32},{32,40},{40,48},{48,56},{56,6... | collective-permute-start | bytes 393224 | tf_op jit(solution)/shard_map/while/body/eval_jaxpr/ppermute | solution.py:12
  96.7 8.1 %collective-permute-start = (bf16[32,2048]{1,0:T(8,128)(2,1)S(1)}, bf16[32,2048]{1,0:T(8,128)(2,1)S(1)}, u32[]{:S(2)}, u32[]{:S(2)}) collective-permute-start(bf16[32,2048]{1,0:T(8,128)(2,1)S(1)} %get-tuple-element.350), channel_id=1, source_target_pairs={{248,0},{0,8},{8,16},{16,24},{24,32},{32,40},{40,48},{48,56},{56,6... | collective-permute-start | bytes 393224 | tf_op jit(solution)/shard_map/while/body/eval_jaxpr/ppermute | solution.py:12
  108.1 8.1 %collective-permute-start = (bf16[32,2048]{1,0:T(8,128)(2,1)S(1)}, bf16[32,2048]{1,0:T(8,128)(2,1)S(1)}, u32[]{:S(2)}, u32[]{:S(2)}) collective-permute-start(bf16[32,2048]{1,0:T(8,128)(2,1)S(1)} %get-tuple-element.350), channel_id=1, source_target_pairs={{248,0},{0,8},{8,16},{16,24},{24,32},{32,40},{40,48},{48,56},{56,6... | collective-permute-start | bytes 393224 | tf_op jit(solution)/shard_map/while/body/eval_jaxpr/ppermute | solution.py:12
  119.5 8.1 %collective-permute-start = (bf16[32,2048]{1,0:T(8,128)(2,1)S(1)}, bf16[32,2048]{1,0:T(8,128)(2,1)S(1)}, u32[]{:S(2)}, u32[]{:S(2)}) collective-permute-start(bf16[32,2048]{1,0:T(8,128)(2,1)S(1)} %get-tuple-element.350), channel_id=1, source_target_pairs={{248,0},{0,8},{8,16},{16,24},{24,32},{32,40},{40,48},{48,56},{56,6... | collective-permute-start | bytes 393224 | tf_op jit(solution)/shard_map/while/body/eval_jaxpr/ppermute | solution.py:12
  130.9 8.1 %collective-permute-start = (bf16[32,2048]{1,0:T(8,128)(2,1)S(1)}, bf16[32,2048]{1,0:T(8,128)(2,1)S(1)}, u32[]{:S(2)}, u32[]{:S(2)}) collective-permute-start(bf16[32,2048]{1,0:T(8,128)(2,1)S(1)} %get-tuple-element.350), channel_id=1, source_target_pairs={{248,0},{0,8},{8,16},{16,24},{24,32},{32,40},{40,48},{48,56},{56,6... | collective-permute-start | bytes 393224 | tf_op jit(solution)/shard_map/while/body/eval_jaxpr/ppermute | solution.py:12
  142.3 8.1 %collective-permute-start = (bf16[32,2048]{1,0:T(8,128)(2,1)S(1)}, bf16[32,2048]{1,0:T(8,128)(2,1)S(1)}, u32[]{:S(2)}, u32[]{:S(2)}) collective-permute-start(bf16[32,2048]{1,0:T(8,128)(2,1)S(1)} %get-tuple-element.350), channel_id=1, source_target_pairs={{248,0},{0,8},{8,16},{16,24},{24,32},{32,40},{40,48},{48,56},{56,6... | collective-permute-start | bytes 393224 | tf_op jit(solution)/shard_map/while/body/eval_jaxpr/ppermute | solution.py:12
  153.7 8.1 %collective-permute-start = (bf16[32,2048]{1,0:T(8,128)(2,1)S(1)}, bf16[32,2048]{1,0:T(8,128)(2,1)S(1)}, u32[]{:S(2)}, u32[]{:S(2)}) collective-permute-start(bf16[32,2048]{1,0:T(8,128)(2,1)S(1)} %get-tuple-element.350), channel_id=1, source_target_pairs={{248,0},{0,8},{8,16},{16,24},{24,32},{32,40},{40,48},{48,56},{56,6... | collective-permute-start | bytes 393224 | tf_op jit(solution)/shard_map/while/body/eval_jaxpr/ppermute | solution.py:12
  165.1 8.1 %collective-permute-start = (bf16[32,2048]{1,0:T(8,128)(2,1)S(1)}, bf16[32,2048]{1,0:T(8,128)(2,1)S(1)}, u32[]{:S(2)}, u32[]{:S(2)}) collective-permute-start(bf16[32,2048]{1,0:T(8,128)(2,1)S(1)} %get-tuple-element.350), channel_id=1, source_target_pairs={{248,0},{0,8},{8,16},{16,24},{24,32},{32,40},{40,48},{48,56},{56,6... | collective-permute-start | bytes 393224 | tf_op jit(solution)/shard_map/while/body/eval_jaxpr/ppermute | solution.py:12
  176.5 8.1 %collective-permute-start = (bf16[32,2048]{1,0:T(8,128)(2,1)S(1)}, bf16[32,2048]{1,0:T(8,128)(2,1)S(1)}, u32[]{:S(2)}, u32[]{:S(2)}) collective-permute-start(bf16[32,2048]{1,0:T(8,128)(2,1)S(1)} %get-tuple-element.350), channel_id=1, source_target_pairs={{248,0},{0,8},{8,16},{16,24},{24,32},{32,40},{40,48},{48,56},{56,6... | collective-permute-start | bytes 393224 | tf_op jit(solution)/shard_map/while/body/eval_jaxpr/ppermute | solution.py:12
  187.9 8.1 %collective-permute-start = (bf16[32,2048]{1,0:T(8,128)(2,1)S(1)}, bf16[32,2048]{1,0:T(8,128)(2,1)S(1)}, u32[]{:S(2)}, u32[]{:S(2)}) collective-permute-start(bf16[32,2048]{1,0:T(8,128)(2,1)S(1)} %get-tuple-element.350), channel_id=1, source_target_pairs={{248,0},{0,8},{8,16},{16,24},{24,32},{32,40},{40,48},{48,56},{56,6... | collective-permute-start | bytes 393224 | tf_op jit(solution)/shard_map/while/body/eval_jaxpr/ppermute | solution.py:12
  199.3 8.1 %collective-permute-start = (bf16[32,2048]{1,0:T(8,128)(2,1)S(1)}, bf16[32,2048]{1,0:T(8,128)(2,1)S(1)}, u32[]{:S(2)}, u32[]{:S(2)}) collective-permute-start(bf16[32,2048]{1,0:T(8,128)(2,1)S(1)} %get-tuple-element.350), channel_id=1, source_target_pairs={{248,0},{0,8},{8,16},{16,24},{24,32},{32,40},{40,48},{48,56},{56,6... | collective-permute-start | bytes 393224 | tf_op jit(solution)/shard_map/while/body/eval_jaxpr/ppermute | solution.py:12
  210.7 8.1 %collective-permute-start = (bf16[32,2048]{1,0:T(8,128)(2,1)S(1)}, bf16[32,2048]{1,0:T(8,128)(2,1)S(1)}, u32[]{:S(2)}, u32[]{:S(2)}) collective-permute-start(bf16[32,2048]{1,0:T(8,128)(2,1)S(1)} %get-tuple-element.350), channel_id=1, source_target_pairs={{248,0},{0,8},{8,16},{16,24},{24,32},{32,40},{40,48},{48,56},{56,6... | collective-permute-start | bytes 393224 | tf_op jit(solution)/shard_map/while/body/eval_jaxpr/ppermute | solution.py:12
  222.1 8.1 %collective-permute-start = (bf16[32,2048]{1,0:T(8,128)(2,1)S(1)}, bf16[32,2048]{1,0:T(8,128)(2,1)S(1)}, u32[]{:S(2)}, u32[]{:S(2)}) collective-permute-start(bf16[32,2048]{1,0:T(8,128)(2,1)S(1)} %get-tuple-element.350), channel_id=1, source_target_pairs={{248,0},{0,8},{8,16},{16,24},{24,32},{32,40},{40,48},{48,56},{56,6... | collective-permute-start | bytes 393224 | tf_op jit(solution)/shard_map/while/body/eval_jaxpr/ppermute | solution.py:12
  233.5 8.1 %collective-permute-start = (bf16[32,2048]{1,0:T(8,128)(2,1)S(1)}, bf16[32,2048]{1,0:T(8,128)(2,1)S(1)}, u32[]{:S(2)}, u32[]{:S(2)}) collective-permute-start(bf16[32,2048]{1,0:T(8,128)(2,1)S(1)} %get-tuple-element.350), channel_id=1, source_target_pairs={{248,0},{0,8},{8,16},{16,24},{24,32},{32,40},{40,48},{48,56},{56,6... | collective-permute-start | bytes 393224 | tf_op jit(solution)/shard_map/while/body/eval_jaxpr/ppermute | solution.py:12
  244.9 8.1 %collective-permute-start = (bf16[32,2048]{1,0:T(8,128)(2,1)S(1)}, bf16[32,2048]{1,0:T(8,128)(2,1)S(1)}, u32[]{:S(2)}, u32[]{:S(2)}) collective-permute-start(bf16[32,2048]{1,0:T(8,128)(2,1)S(1)} %get-tuple-element.350), channel_id=1, source_target_pairs={{248,0},{0,8},{8,16},{16,24},{24,32},{32,40},{40,48},{48,56},{56,6... | collective-permute-start | bytes 393224 | tf_op jit(solution)/shard_map/while/body/eval_jaxpr/ppermute | solution.py:12
  256.3 8.1 %collective-permute-start = (bf16[32,2048]{1,0:T(8,128)(2,1)S(1)}, bf16[32,2048]{1,0:T(8,128)(2,1)S(1)}, u32[]{:S(2)}, u32[]{:S(2)}) collective-permute-start(bf16[32,2048]{1,0:T(8,128)(2,1)S(1)} %get-tuple-element.350), channel_id=1, source_target_pairs={{248,0},{0,8},{8,16},{16,24},{24,32},{32,40},{40,48},{48,56},{56,6... | collective-permute-start | bytes 393224 | tf_op jit(solution)/shard_map/while/body/eval_jaxpr/ppermute | solution.py:12
  267.7 8.1 %collective-permute-start = (bf16[32,2048]{1,0:T(8,128)(2,1)S(1)}, bf16[32,2048]{1,0:T(8,128)(2,1)S(1)}, u32[]{:S(2)}, u32[]{:S(2)}) collective-permute-start(bf16[32,2048]{1,0:T(8,128)(2,1)S(1)} %get-tuple-element.350), channel_id=1, source_target_pairs={{248,0},{0,8},{8,16},{16,24},{24,32},{32,40},{40,48},{48,56},{56,6... | collective-permute-start | bytes 393224 | tf_op jit(solution)/shard_map/while/body/eval_jaxpr/ppermute | solution.py:12
  279.1 8.1 %collective-permute-start = (bf16[32,2048]{1,0:T(8,128)(2,1)S(1)}, bf16[32,2048]{1,0:T(8,128)(2,1)S(1)}, u32[]{:S(2)}, u32[]{:S(2)}) collective-permute-start(bf16[32,2048]{1,0:T(8,128)(2,1)S(1)} %get-tuple-element.350), channel_id=1, source_target_pairs={{248,0},{0,8},{8,16},{16,24},{24,32},{32,40},{40,48},{48,56},{56,6... | collective-permute-start | bytes 393224 | tf_op jit(solution)/shard_map/while/body/eval_jaxpr/ppermute | solution.py:12
  290.5 8.1 %collective-permute-start = (bf16[32,2048]{1,0:T(8,128)(2,1)S(1)}, bf16[32,2048]{1,0:T(8,128)(2,1)S(1)}, u32[]{:S(2)}, u32[]{:S(2)}) collective-permute-start(bf16[32,2048]{1,0:T(8,128)(2,1)S(1)} %get-tuple-element.350), channel_id=1, source_target_pairs={{248,0},{0,8},{8,16},{16,24},{24,32},{32,40},{40,48},{48,56},{56,6... | collective-permute-start | bytes 393224 | tf_op jit(solution)/shard_map/while/body/eval_jaxpr/ppermute | solution.py:12
  301.9 8.1 %collective-permute-start = (bf16[32,2048]{1,0:T(8,128)(2,1)S(1)}, bf16[32,2048]{1,0:T(8,128)(2,1)S(1)}, u32[]{:S(2)}, u32[]{:S(2)}) collective-permute-start(bf16[32,2048]{1,0:T(8,128)(2,1)S(1)} %get-tuple-element.350), channel_id=1, source_target_pairs={{248,0},{0,8},{8,16},{16,24},{24,32},{32,40},{40,48},{48,56},{56,6... | collective-permute-start | bytes 393224 | tf_op jit(solution)/shard_map/while/body/eval_jaxpr/ppermute | solution.py:12
  313.3 8.1 %collective-permute-start = (bf16[32,2048]{1,0:T(8,128)(2,1)S(1)}, bf16[32,2048]{1,0:T(8,128)(2,1)S(1)}, u32[]{:S(2)}, u32[]{:S(2)}) collective-permute-start(bf16[32,2048]{1,0:T(8,128)(2,1)S(1)} %get-tuple-element.350), channel_id=1, source_target_pairs={{248,0},{0,8},{8,16},{16,24},{24,32},{32,40},{40,48},{48,56},{56,6... | collective-permute-start | bytes 393224 | tf_op jit(solution)/shard_map/while/body/eval_jaxpr/ppermute | solution.py:12
  324.7 8.1 %collective-permute-start = (bf16[32,2048]{1,0:T(8,128)(2,1)S(1)}, bf16[32,2048]{1,0:T(8,128)(2,1)S(1)}, u32[]{:S(2)}, u32[]{:S(2)}) collective-permute-start(bf16[32,2048]{1,0:T(8,128)(2,1)S(1)} %get-tuple-element.350), channel_id=1, source_target_pairs={{248,0},{0,8},{8,16},{16,24},{24,32},{32,40},{40,48},{48,56},{56,6... | collective-permute-start | bytes 393224 | tf_op jit(solution)/shard_map/while/body/eval_jaxpr/ppermute | solution.py:12
  336.2 8.1 %collective-permute-start = (bf16[32,2048]{1,0:T(8,128)(2,1)S(1)}, bf16[32,2048]{1,0:T(8,128)(2,1)S(1)}, u32[]{:S(2)}, u32[]{:S(2)}) collective-permute-start(bf16[32,2048]{1,0:T(8,128)(2,1)S(1)} %get-tuple-element.350), channel_id=1, source_target_pairs={{248,0},{0,8},{8,16},{16,24},{24,32},{32,40},{40,48},{48,56},{56,6... | collective-permute-start | bytes 393224 | tf_op jit(solution)/shard_map/while/body/eval_jaxpr/ppermute | solution.py:12
  347.6 8.1 %collective-permute-start = (bf16[32,2048]{1,0:T(8,128)(2,1)S(1)}, bf16[32,2048]{1,0:T(8,128)(2,1)S(1)}, u32[]{:S(2)}, u32[]{:S(2)}) collective-permute-start(bf16[32,2048]{1,0:T(8,128)(2,1)S(1)} %get-tuple-element.350), channel_id=1, source_target_pairs={{248,0},{0,8},{8,16},{16,24},{24,32},{32,40},{40,48},{48,56},{56,6... | collective-permute-start | bytes 393224 | tf_op jit(solution)/shard_map/while/body/eval_jaxpr/ppermute | solution.py:12
Sparse Core Ops, SparseCore 0:
  359.8 52.0 all-gather.1
where the time goes:
time: 424 us; the launch traced here: 421 us
  waiting for transfers between devices  178 us (42%)
  other arithmetic  130 us (31%)
  matrix products  49.1 us (12%)
  local copies, waits for them, and re-layouts  20.5 us (5%)
  loops' own time  19.7 us (5%)
  between operations  14.7 us (3%)
  starting transfers between devices  9.36 us (2%)
    ppermute x31, waiting for transfers between devices, shifted(): return lax.ppermute(block, axis, route)  125 us
    all_gather x1, waiting for transfers between devices, body(): lax.all_gather(rounded, 'feat', axis=0, tiled=True)  52.2 us
    dot_general x32, matrix products, add_tiles(): jnp.einsum('hwj,wij->hwi', picked, tile_group, preferred_element_type=jnp...  46.8 us
    reduce_sum x32, other arithmetic, add_slab(): before = jnp.sum(((source_slab < slab_index) & usable).astype(jnp.int32))  40.1 us
    scatter-add x32, other arithmetic, add_tiles(): return totals.at[:, target_blocks, :].add(masked)  38.7 us
    select_n x32, other arithmetic, add_tiles(): return totals.at[:, target_blocks, :].add(masked)  24.1 us
    and x32, other arithmetic, add_slab(): (source_slab == slab_index) & usable  20.8 us
    another operation x1, loops' own time, body(): lax.fori_loop(1, slab_count, forward_turn, (add_slab(zero_totals, feature...  19.7 us
  transfers between devices with their start and end apart: 32, of which 32 were waited for; matrix products, arithmetic and copies ran while one was open for 21% of the time, Pallas kernels for 0%

commit v1 on v0

--- a/solution.py
+++ b/solution.py
@@ -60,7 +60,9 @@
     combined = jnp.einsum(
         "ko,kn->on",
         columns,
-        lax.all_gather(rounded, "feat", axis=0, tiled=True),
+        jnp.concatenate(
+            lax.all_to_all(jnp.stack([rounded] * lax.axis_size("feat")), "feat", 0, 0), axis=0
+        ),
         preferred_element_type=jnp.float32,
     )
     return jnp.maximum(combined, 0.0).astype(jnp.bfloat16)

time: 424 us -> 385 us (0.908)
  the two profiles are of different devices: /device:TPU:4 before, /device:TPU:2 now
where the time goes in v1:
time: 385 us; the launch traced here: 382 us
  waiting for transfers between devices  153 us (40%)
  other arithmetic  130 us (34%)
  matrix products  47.8 us (12%)
  local copies, waits for them, and re-layouts  21.6 us (6%)
  loops' own time  19.8 us (5%)
  starting transfers between devices  8.51 us (2%)
    ppermute x31, waiting for transfers between devices, shifted(): return lax.ppermute(block, axis, route)  143 us
    dot_general x32, matrix products, add_tiles(): jnp.einsum('hwj,wij->hwi', picked, tile_group, preferred_element_type=jnp...  46.8 us
    reduce_sum x32, other arithmetic, add_slab(): before = jnp.sum(((source_slab < slab_index) & usable).astype(jnp.int32))  40.1 us
    scatter-add x32, other arithmetic, add_tiles(): return totals.at[:, target_blocks, :].add(masked)  38.7 us
    select_n x32, other arithmetic, add_tiles(): return totals.at[:, target_blocks, :].add(masked)  24.1 us
    and x32, other arithmetic, add_slab(): (source_slab == slab_index) & usable  20.8 us
    another operation x1, loops' own time, body(): lax.fori_loop(1, slab_count, forward_turn, (add_slab(zero_totals, feature...  19.8 us
    gather x32, local copies, waits for them, and re-layouts, add_tiles(): picked = jnp.take(blocks, source_blocks, axis=1)  18.4 us
  transfers between devices with their start and end apart: 32, of which 32 were waited for; matrix products, arithmetic and copies ran while one was open for 23% of the time, Pallas kernels for 0%

profile of v1, /device:TPU:2, one launch (start us, length us, event | category | flops | bytes accessed | tf_op | source)
XLA Modules:
  0.0 381.7 jit_solution(12770760089464473410)
XLA Ops:
  8.4 355.1 %while.18 = (s32[]{:T(128)}, f32[32,16,128]{2,0,1:T(8,128)S(1)}, bf16[32,2048]{1,0:T(8,128)(2,1)S(1)}, s32[]{:T(128)}, s32[256]{0:T(256)S(1)}, /*index=5*/s32[25...) while((s32[]{:T(128)}, f32[32,16,128]{2,0,1:T(8,128)S(1)}, ...), condition=%wide.region_5.7_spmd.clone, body=%wide.region_2.6_spmd.clone.sunk | while | flops 16977072 | bytes 3022064 | solution.py:53
  12.0 6.1 %collective-permute-done = bf16[32,2048]{1,0:T(8,128)(2,1)S(1)} collective-permute-done((bf16[32,2048]{1,0:T(8,128)(2,1)S(1)}, bf16[32,2048]{1,0:T(8,128)(2,1)S(1)}, u32[]{:S(2)}, u32[]{:S(2)}) %collective-permute-start) | collective-permute-done | bytes 131104 | tf_op jit(solution)/shard_map/while/body/eval_jaxpr/ppermute | solution.py:12
  18.6 1.5 fusion.35
  24.9 4.6 %collective-permute-done = bf16[32,2048]{1,0:T(8,128)(2,1)S(1)} collective-permute-done((bf16[32,2048]{1,0:T(8,128)(2,1)S(1)}, bf16[32,2048]{1,0:T(8,128)(2,1)S(1)}, u32[]{:S(2)}, u32[]{:S(2)}) %collective-permute-start) | collective-permute-done | bytes 131104 | tf_op jit(solution)/shard_map/while/body/eval_jaxpr/ppermute | solution.py:12
  30.0 1.5 fusion.35
  36.3 4.6 %collective-permute-done = bf16[32,2048]{1,0:T(8,128)(2,1)S(1)} collective-permute-done((bf16[32,2048]{1,0:T(8,128)(2,1)S(1)}, bf16[32,2048]{1,0:T(8,128)(2,1)S(1)}, u32[]{:S(2)}, u32[]{:S(2)}) %collective-permute-start) | collective-permute-done | bytes 131104 | tf_op jit(solution)/shard_map/while/body/eval_jaxpr/ppermute | solution.py:12
  41.4 1.5 fusion.35
  47.7 4.6 %collective-permute-done = bf16[32,2048]{1,0:T(8,128)(2,1)S(1)} collective-permute-done((bf16[32,2048]{1,0:T(8,128)(2,1)S(1)}, bf16[32,2048]{1,0:T(8,128)(2,1)S(1)}, u32[]{:S(2)}, u32[]{:S(2)}) %collective-permute-start) | collective-permute-done | bytes 131104 | tf_op jit(solution)/shard_map/while/body/eval_jaxpr/ppermute | solution.py:12
  52.8 1.5 fusion.35
  59.1 4.6 %collective-permute-done = bf16[32,2048]{1,0:T(8,128)(2,1)S(1)} collective-permute-done((bf16[32,2048]{1,0:T(8,128)(2,1)S(1)}, bf16[32,2048]{1,0:T(8,128)(2,1)S(1)}, u32[]{:S(2)}, u32[]{:S(2)}) %collective-permute-start) | collective-permute-done | bytes 131104 | tf_op jit(solution)/shard_map/while/body/eval_jaxpr/ppermute | solution.py:12
  64.2 1.5 fusion.35
  70.5 4.6 %collective-permute-done = bf16[32,2048]{1,0:T(8,128)(2,1)S(1)} collective-permute-done((bf16[32,2048]{1,0:T(8,128)(2,1)S(1)}, bf16[32,2048]{1,0:T(8,128)(2,1)S(1)}, u32[]{:S(2)}, u32[]{:S(2)}) %collective-permute-start) | collective-permute-done | bytes 131104 | tf_op jit(solution)/shard_map/while/body/eval_jaxpr/ppermute | solution.py:12
  75.6 1.5 fusion.35
  81.9 4.6 %collective-permute-done = bf16[32,2048]{1,0:T(8,128)(2,1)S(1)} collective-permute-done((bf16[32,2048]{1,0:T(8,128)(2,1)S(1)}, bf16[32,2048]{1,0:T(8,128)(2,1)S(1)}, u32[]{:S(2)}, u32[]{:S(2)}) %collective-permute-start) | collective-permute-done | bytes 131104 | tf_op jit(solution)/shard_map/while/body/eval_jaxpr/ppermute | solution.py:12
  87.0 1.5 fusion.35
  93.3 4.6 %collective-permute-done = bf16[32,2048]{1,0:T(8,128)(2,1)S(1)} collective-permute-done((bf16[32,2048]{1,0:T(8,128)(2,1)S(1)}, bf16[32,2048]{1,0:T(8,128)(2,1)S(1)}, u32[]{:S(2)}, u32[]{:S(2)}) %collective-permute-start) | collective-permute-done | bytes 131104 | tf_op jit(solution)/shard_map/while/body/eval_jaxpr/ppermute | solution.py:12
  98.4 1.5 fusion.35
  104.7 4.6 %collective-permute-done = bf16[32,2048]{1,0:T(8,128)(2,1)S(1)} collective-permute-done((bf16[32,2048]{1,0:T(8,128)(2,1)S(1)}, bf16[32,2048]{1,0:T(8,128)(2,1)S(1)}, u32[]{:S(2)}, u32[]{:S(2)}) %collective-permute-start) | collective-permute-done | bytes 131104 | tf_op jit(solution)/shard_map/while/body/eval_jaxpr/ppermute | solution.py:12
  109.8 1.5 fusion.35
  116.1 4.6 %collective-permute-done = bf16[32,2048]{1,0:T(8,128)(2,1)S(1)} collective-permute-done((bf16[32,2048]{1,0:T(8,128)(2,1)S(1)}, bf16[32,2048]{1,0:T(8,128)(2,1)S(1)}, u32[]{:S(2)}, u32[]{:S(2)}) %collective-permute-start) | collective-permute-done | bytes 131104 | tf_op jit(solution)/shard_map/while/body/eval_jaxpr/ppermute | solution.py:12
  121.2 1.5 fusion.35
  127.5 4.6 %collective-permute-done = bf16[32,2048]{1,0:T(8,128)(2,1)S(1)} collective-permute-done((bf16[32,2048]{1,0:T(8,128)(2,1)S(1)}, bf16[32,2048]{1,0:T(8,128)(2,1)S(1)}, u32[]{:S(2)}, u32[]{:S(2)}) %collective-permute-start) | collective-permute-done | bytes 131104 | tf_op jit(solution)/shard_map/while/body/eval_jaxpr/ppermute | solution.py:12
  132.6 1.5 fusion.35
  138.9 4.6 %collective-permute-done = bf16[32,2048]{1,0:T(8,128)(2,1)S(1)} collective-permute-done((bf16[32,2048]{1,0:T(8,128)(2,1)S(1)}, bf16[32,2048]{1,0:T(8,128)(2,1)S(1)}, u32[]{:S(2)}, u32[]{:S(2)}) %collective-permute-start) | collective-permute-done | bytes 131104 | tf_op jit(solution)/shard_map/while/body/eval_jaxpr/ppermute | solution.py:12
  144.0 1.5 fusion.35
  150.3 4.6 %collective-permute-done = bf16[32,2048]{1,0:T(8,128)(2,1)S(1)} collective-permute-done((bf16[32,2048]{1,0:T(8,128)(2,1)S(1)}, bf16[32,2048]{1,0:T(8,128)(2,1)S(1)}, u32[]{:S(2)}, u32[]{:S(2)}) %collective-permute-start) | collective-permute-done | bytes 131104 | tf_op jit(solution)/shard_map/while/body/eval_jaxpr/ppermute | solution.py:12
  155.4 1.5 fusion.35
  161.7 4.6 %collective-permute-done = bf16[32,2048]{1,0:T(8,128)(2,1)S(1)} collective-permute-done((bf16[32,2048]{1,0:T(8,128)(2,1)S(1)}, bf16[32,2048]{1,0:T(8,128)(2,1)S(1)}, u32[]{:S(2)}, u32[]{:S(2)}) %collective-permute-start) | collective-permute-done | bytes 131104 | tf_op jit(solution)/shard_map/while/body/eval_jaxpr/ppermute | solution.py:12
  166.8 1.5 fusion.35
  173.1 4.6 %collective-permute-done = bf16[32,2048]{1,0:T(8,128)(2,1)S(1)} collective-permute-done((bf16[32,2048]{1,0:T(8,128)(2,1)S(1)}, bf16[32,2048]{1,0:T(8,128)(2,1)S(1)}, u32[]{:S(2)}, u32[]{:S(2)}) %collective-permute-start) | collective-permute-done | bytes 131104 | tf_op jit(solution)/shard_map/while/body/eval_jaxpr/ppermute | solution.py:12
  178.2 1.5 fusion.35
  184.5 4.6 %collective-permute-done = bf16[32,2048]{1,0:T(8,128)(2,1)S(1)} collective-permute-done((bf16[32,2048]{1,0:T(8,128)(2,1)S(1)}, bf16[32,2048]{1,0:T(8,128)(2,1)S(1)}, u32[]{:S(2)}, u32[]{:S(2)}) %collective-permute-start) | collective-permute-done | bytes 131104 | tf_op jit(solution)/shard_map/while/body/eval_jaxpr/ppermute | solution.py:12
  189.6 1.5 fusion.35
  195.9 4.6 %collective-permute-done = bf16[32,2048]{1,0:T(8,128)(2,1)S(1)} collective-permute-done((bf16[32,2048]{1,0:T(8,128)(2,1)S(1)}, bf16[32,2048]{1,0:T(8,128)(2,1)S(1)}, u32[]{:S(2)}, u32[]{:S(2)}) %collective-permute-start) | collective-permute-done | bytes 131104 | tf_op jit(solution)/shard_map/while/body/eval_jaxpr/ppermute | solution.py:12
  201.0 1.5 fusion.35
  207.3 4.6 %collective-permute-done = bf16[32,2048]{1,0:T(8,128)(2,1)S(1)} collective-permute-done((bf16[32,2048]{1,0:T(8,128)(2,1)S(1)}, bf16[32,2048]{1,0:T(8,128)(2,1)S(1)}, u32[]{:S(2)}, u32[]{:S(2)}) %collective-permute-start) | collective-permute-done | bytes 131104 | tf_op jit(solution)/shard_map/while/body/eval_jaxpr/ppermute | solution.py:12
  212.4 1.5 fusion.35
  218.7 4.6 %collective-permute-done = bf16[32,2048]{1,0:T(8,128)(2,1)S(1)} collective-permute-done((bf16[32,2048]{1,0:T(8,128)(2,1)S(1)}, bf16[32,2048]{1,0:T(8,128)(2,1)S(1)}, u32[]{:S(2)}, u32[]{:S(2)}) %collective-permute-start) | collective-permute-done | bytes 131104 | tf_op jit(solution)/shard_map/while/body/eval_jaxpr/ppermute | solution.py:12
  223.8 1.5 fusion.35
  230.1 4.6 %collective-permute-done = bf16[32,2048]{1,0:T(8,128)(2,1)S(1)} collective-permute-done((bf16[32,2048]{1,0:T(8,128)(2,1)S(1)}, bf16[32,2048]{1,0:T(8,128)(2,1)S(1)}, u32[]{:S(2)}, u32[]{:S(2)}) %collective-permute-start) | collective-permute-done | bytes 131104 | tf_op jit(solution)/shard_map/while/body/eval_jaxpr/ppermute | solution.py:12
  235.2 1.5 fusion.35
  241.5 4.6 %collective-permute-done = bf16[32,2048]{1,0:T(8,128)(2,1)S(1)} collective-permute-done((bf16[32,2048]{1,0:T(8,128)(2,1)S(1)}, bf16[32,2048]{1,0:T(8,128)(2,1)S(1)}, u32[]{:S(2)}, u32[]{:S(2)}) %collective-permute-start) | collective-permute-done | bytes 131104 | tf_op jit(solution)/shard_map/while/body/eval_jaxpr/ppermute | solution.py:12
  246.7 1.5 fusion.35
  252.9 4.6 %collective-permute-done = bf16[32,2048]{1,0:T(8,128)(2,1)S(1)} collective-permute-done((bf16[32,2048]{1,0:T(8,128)(2,1)S(1)}, bf16[32,2048]{1,0:T(8,128)(2,1)S(1)}, u32[]{:S(2)}, u32[]{:S(2)}) %collective-permute-start) | collective-permute-done | bytes 131104 | tf_op jit(solution)/shard_map/while/body/eval_jaxpr/ppermute | solution.py:12
  258.1 1.5 fusion.35
  264.3 4.6 %collective-permute-done = bf16[32,2048]{1,0:T(8,128)(2,1)S(1)} collective-permute-done((bf16[32,2048]{1,0:T(8,128)(2,1)S(1)}, bf16[32,2048]{1,0:T(8,128)(2,1)S(1)}, u32[]{:S(2)}, u32[]{:S(2)}) %collective-permute-start) | collective-permute-done | bytes 131104 | tf_op jit(solution)/shard_map/while/body/eval_jaxpr/ppermute | solution.py:12
  269.5 1.5 fusion.35
  275.7 4.6 %collective-permute-done = bf16[32,2048]{1,0:T(8,128)(2,1)S(1)} collective-permute-done((bf16[32,2048]{1,0:T(8,128)(2,1)S(1)}, bf16[32,2048]{1,0:T(8,128)(2,1)S(1)}, u32[]{:S(2)}, u32[]{:S(2)}) %collective-permute-start) | collective-permute-done | bytes 131104 | tf_op jit(solution)/shard_map/while/body/eval_jaxpr/ppermute | solution.py:12
  280.9 1.5 fusion.35
  287.1 4.6 %collective-permute-done = bf16[32,2048]{1,0:T(8,128)(2,1)S(1)} collective-permute-done((bf16[32,2048]{1,0:T(8,128)(2,1)S(1)}, bf16[32,2048]{1,0:T(8,128)(2,1)S(1)}, u32[]{:S(2)}, u32[]{:S(2)}) %collective-permute-start) | collective-permute-done | bytes 131104 | tf_op jit(solution)/shard_map/while/body/eval_jaxpr/ppermute | solution.py:12
  292.3 1.5 fusion.35
  298.5 4.6 %collective-permute-done = bf16[32,2048]{1,0:T(8,128)(2,1)S(1)} collective-permute-done((bf16[32,2048]{1,0:T(8,128)(2,1)S(1)}, bf16[32,2048]{1,0:T(8,128)(2,1)S(1)}, u32[]{:S(2)}, u32[]{:S(2)}) %collective-permute-start) | collective-permute-done | bytes 131104 | tf_op jit(solution)/shard_map/while/body/eval_jaxpr/ppermute | solution.py:12
  303.7 1.5 fusion.35
  309.9 4.6 %collective-permute-done = bf16[32,2048]{1,0:T(8,128)(2,1)S(1)} collective-permute-done((bf16[32,2048]{1,0:T(8,128)(2,1)S(1)}, bf16[32,2048]{1,0:T(8,128)(2,1)S(1)}, u32[]{:S(2)}, u32[]{:S(2)}) %collective-permute-start) | collective-permute-done | bytes 131104 | tf_op jit(solution)/shard_map/while/body/eval_jaxpr/ppermute | solution.py:12
  315.1 1.5 fusion.35
  321.3 4.6 %collective-permute-done = bf16[32,2048]{1,0:T(8,128)(2,1)S(1)} collective-permute-done((bf16[32,2048]{1,0:T(8,128)(2,1)S(1)}, bf16[32,2048]{1,0:T(8,128)(2,1)S(1)}, u32[]{:S(2)}, u32[]{:S(2)}) %collective-permute-start) | collective-permute-done | bytes 131104 | tf_op jit(solution)/shard_map/while/body/eval_jaxpr/ppermute | solution.py:12
  326.5 1.5 fusion.35
  332.7 4.6 %collective-permute-done = bf16[32,2048]{1,0:T(8,128)(2,1)S(1)} collective-permute-done((bf16[32,2048]{1,0:T(8,128)(2,1)S(1)}, bf16[32,2048]{1,0:T(8,128)(2,1)S(1)}, u32[]{:S(2)}, u32[]{:S(2)}) %collective-permute-start) | collective-permute-done | bytes 131104 | tf_op jit(solution)/shard_map/while/body/eval_jaxpr/ppermute | solution.py:12
  337.9 1.5 fusion.35
  344.1 4.6 %collective-permute-done = bf16[32,2048]{1,0:T(8,128)(2,1)S(1)} collective-permute-done((bf16[32,2048]{1,0:T(8,128)(2,1)S(1)}, bf16[32,2048]{1,0:T(8,128)(2,1)S(1)}, u32[]{:S(2)}, u32[]{:S(2)}) %collective-permute-start) | collective-permute-done | bytes 131104 | tf_op jit(solution)/shard_map/while/body/eval_jaxpr/ppermute | solution.py:12
  349.3 1.5 fusion.35
  355.5 4.7 %collective-permute-done = bf16[32,2048]{1,0:T(8,128)(2,1)S(1)} collective-permute-done((bf16[32,2048]{1,0:T(8,128)(2,1)S(1)}, bf16[32,2048]{1,0:T(8,128)(2,1)S(1)}, u32[]{:S(2)}, u32[]{:S(2)}) %collective-permute-start) | collective-permute-done | bytes 131104 | tf_op jit(solution)/shard_map/while/body/eval_jaxpr/ppermute | solution.py:12
  364.7 5.9 %all-to-all-start = ((bf16[8,32,2048]{2,1,0:T(8,128)(2,1)}), bf16[8,32,2048]{2,1,0:T(8,128)(2,1)S(1)}, u32[]{:S(2)}, u32[]{:S(2)}) async-start(bf16[8,32,2048]{2,1,0:T(8,128)(2,1)} %stack.2), calls=%async_computation | async-start | bytes 2097152 | tf_op jit(solution)/shard_map/all_to_all | solution.py:64
  370.6 10.0 %all-to-all-done = bf16[8,32,2048]{2,1,0:T(8,128)(2,1)S(1)} async-done(((bf16[8,32,2048]{2,1,0:T(8,128)(2,1)}), bf16[8,32,2048]{2,1,0:T(8,128)(2,1)S(1)}, u32[]{:S(2)}, u32[]{:S(2)}) %all-to-all-start) | async-done | bytes 1048608 | tf_op jit(solution)/shard_map/all_to_all | solution.py:64
  (359 shorter events, 157.7 us)
Async XLA Ops:
  0.0 380.6 %copy-start = (bf16[256,256]{1,0:T(8,128)(2,1)S(1)}, bf16[256,256]{1,0:T(8,128)(2,1)}, u32[]{:S(2)}) copy-start(bf16[256,256]{1,0:T(8,128)(2,1)} %param.15) | copy-start | bytes 393220
  8.5 9.6 %collective-permute-start = (bf16[32,2048]{1,0:T(8,128)(2,1)S(1)}, bf16[32,2048]{1,0:T(8,128)(2,1)S(1)}, u32[]{:S(2)}, u32[]{:S(2)}) collective-permute-start(bf16[32,2048]{1,0:T(8,128)(2,1)S(1)} %get-tuple-element.350), channel_id=1, source_target_pairs={{248,0},{0,8},{8,16},{16,24},{24,32},{32,40},{40,48},{48,56},{56,6... | collective-permute-start | bytes 393224 | tf_op jit(solution)/shard_map/while/body/eval_jaxpr/ppermute | solution.py:12
  21.4 8.1 %collective-permute-start = (bf16[32,2048]{1,0:T(8,128)(2,1)S(1)}, bf16[32,2048]{1,0:T(8,128)(2,1)S(1)}, u32[]{:S(2)}, u32[]{:S(2)}) collective-permute-start(bf16[32,2048]{1,0:T(8,128)(2,1)S(1)} %get-tuple-element.350), channel_id=1, source_target_pairs={{248,0},{0,8},{8,16},{16,24},{24,32},{32,40},{40,48},{48,56},{56,6... | collective-permute-start | bytes 393224 | tf_op jit(solution)/shard_map/while/body/eval_jaxpr/ppermute | solution.py:12
  32.8 8.1 %collective-permute-start = (bf16[32,2048]{1,0:T(8,128)(2,1)S(1)}, bf16[32,2048]{1,0:T(8,128)(2,1)S(1)}, u32[]{:S(2)}, u32[]{:S(2)}) collective-permute-start(bf16[32,2048]{1,0:T(8,128)(2,1)S(1)} %get-tuple-element.350), channel_id=1, source_target_pairs={{248,0},{0,8},{8,16},{16,24},{24,32},{32,40},{40,48},{48,56},{56,6... | collective-permute-start | bytes 393224 | tf_op jit(solution)/shard_map/while/body/eval_jaxpr/ppermute | solution.py:12
  44.2 8.1 %collective-permute-start = (bf16[32,2048]{1,0:T(8,128)(2,1)S(1)}, bf16[32,2048]{1,0:T(8,128)(2,1)S(1)}, u32[]{:S(2)}, u32[]{:S(2)}) collective-permute-start(bf16[32,2048]{1,0:T(8,128)(2,1)S(1)} %get-tuple-element.350), channel_id=1, source_target_pairs={{248,0},{0,8},{8,16},{16,24},{24,32},{32,40},{40,48},{48,56},{56,6... | collective-permute-start | bytes 393224 | tf_op jit(solution)/shard_map/while/body/eval_jaxpr/ppermute | solution.py:12
  55.6 8.1 %collective-permute-start = (bf16[32,2048]{1,0:T(8,128)(2,1)S(1)}, bf16[32,2048]{1,0:T(8,128)(2,1)S(1)}, u32[]{:S(2)}, u32[]{:S(2)}) collective-permute-start(bf16[32,2048]{1,0:T(8,128)(2,1)S(1)} %get-tuple-element.350), channel_id=1, source_target_pairs={{248,0},{0,8},{8,16},{16,24},{24,32},{32,40},{40,48},{48,56},{56,6... | collective-permute-start | bytes 393224 | tf_op jit(solution)/shard_map/while/body/eval_jaxpr/ppermute | solution.py:12
  67.0 8.1 %collective-permute-start = (bf16[32,2048]{1,0:T(8,128)(2,1)S(1)}, bf16[32,2048]{1,0:T(8,128)(2,1)S(1)}, u32[]{:S(2)}, u32[]{:S(2)}) collective-permute-start(bf16[32,2048]{1,0:T(8,128)(2,1)S(1)} %get-tuple-element.350), channel_id=1, source_target_pairs={{248,0},{0,8},{8,16},{16,24},{24,32},{32,40},{40,48},{48,56},{56,6... | collective-permute-start | bytes 393224 | tf_op jit(solution)/shard_map/while/body/eval_jaxpr/ppermute | solution.py:12
  78.4 8.1 %collective-permute-start = (bf16[32,2048]{1,0:T(8,128)(2,1)S(1)}, bf16[32,2048]{1,0:T(8,128)(2,1)S(1)}, u32[]{:S(2)}, u32[]{:S(2)}) collective-permute-start(bf16[32,2048]{1,0:T(8,128)(2,1)S(1)} %get-tuple-element.350), channel_id=1, source_target_pairs={{248,0},{0,8},{8,16},{16,24},{24,32},{32,40},{40,48},{48,56},{56,6... | collective-permute-start | bytes 393224 | tf_op jit(solution)/shard_map/while/body/eval_jaxpr/ppermute | solution.py:12
  89.8 8.1 %collective-permute-start = (bf16[32,2048]{1,0:T(8,128)(2,1)S(1)}, bf16[32,2048]{1,0:T(8,128)(2,1)S(1)}, u32[]{:S(2)}, u32[]{:S(2)}) collective-permute-start(bf16[32,2048]{1,0:T(8,128)(2,1)S(1)} %get-tuple-element.350), channel_id=1, source_target_pairs={{248,0},{0,8},{8,16},{16,24},{24,32},{32,40},{40,48},{48,56},{56,6... | collective-permute-start | bytes 393224 | tf_op jit(solution)/shard_map/while/body/eval_jaxpr/ppermute | solution.py:12
  101.2 8.1 %collective-permute-start = (bf16[32,2048]{1,0:T(8,128)(2,1)S(1)}, bf16[32,2048]{1,0:T(8,128)(2,1)S(1)}, u32[]{:S(2)}, u32[]{:S(2)}) collective-permute-start(bf16[32,2048]{1,0:T(8,128)(2,1)S(1)} %get-tuple-element.350), channel_id=1, source_target_pairs={{248,0},{0,8},{8,16},{16,24},{24,32},{32,40},{40,48},{48,56},{56,6... | collective-permute-start | bytes 393224 | tf_op jit(solution)/shard_map/while/body/eval_jaxpr/ppermute | solution.py:12
  112.6 8.1 %collective-permute-start = (bf16[32,2048]{1,0:T(8,128)(2,1)S(1)}, bf16[32,2048]{1,0:T(8,128)(2,1)S(1)}, u32[]{:S(2)}, u32[]{:S(2)}) collective-permute-start(bf16[32,2048]{1,0:T(8,128)(2,1)S(1)} %get-tuple-element.350), channel_id=1, source_target_pairs={{248,0},{0,8},{8,16},{16,24},{24,32},{32,40},{40,48},{48,56},{56,6... | collective-permute-start | bytes 393224 | tf_op jit(solution)/shard_map/while/body/eval_jaxpr/ppermute | solution.py:12
  124.0 8.1 %collective-permute-start = (bf16[32,2048]{1,0:T(8,128)(2,1)S(1)}, bf16[32,2048]{1,0:T(8,128)(2,1)S(1)}, u32[]{:S(2)}, u32[]{:S(2)}) collective-permute-start(bf16[32,2048]{1,0:T(8,128)(2,1)S(1)} %get-tuple-element.350), channel_id=1, source_target_pairs={{248,0},{0,8},{8,16},{16,24},{24,32},{32,40},{40,48},{48,56},{56,6... | collective-permute-start | bytes 393224 | tf_op jit(solution)/shard_map/while/body/eval_jaxpr/ppermute | solution.py:12
  135.4 8.1 %collective-permute-start = (bf16[32,2048]{1,0:T(8,128)(2,1)S(1)}, bf16[32,2048]{1,0:T(8,128)(2,1)S(1)}, u32[]{:S(2)}, u32[]{:S(2)}) collective-permute-start(bf16[32,2048]{1,0:T(8,128)(2,1)S(1)} %get-tuple-element.350), channel_id=1, source_target_pairs={{248,0},{0,8},{8,16},{16,24},{24,32},{32,40},{40,48},{48,56},{56,6... | collective-permute-start | bytes 393224 | tf_op jit(solution)/shard_map/while/body/eval_jaxpr/ppermute | solution.py:12
  146.8 8.1 %collective-permute-start = (bf16[32,2048]{1,0:T(8,128)(2,1)S(1)}, bf16[32,2048]{1,0:T(8,128)(2,1)S(1)}, u32[]{:S(2)}, u32[]{:S(2)}) collective-permute-start(bf16[32,2048]{1,0:T(8,128)(2,1)S(1)} %get-tuple-element.350), channel_id=1, source_target_pairs={{248,0},{0,8},{8,16},{16,24},{24,32},{32,40},{40,48},{48,56},{56,6... | collective-permute-start | bytes 393224 | tf_op jit(solution)/shard_map/while/body/eval_jaxpr/ppermute | solution.py:12
  158.2 8.1 %collective-permute-start = (bf16[32,2048]{1,0:T(8,128)(2,1)S(1)}, bf16[32,2048]{1,0:T(8,128)(2,1)S(1)}, u32[]{:S(2)}, u32[]{:S(2)}) collective-permute-start(bf16[32,2048]{1,0:T(8,128)(2,1)S(1)} %get-tuple-element.350), channel_id=1, source_target_pairs={{248,0},{0,8},{8,16},{16,24},{24,32},{32,40},{40,48},{48,56},{56,6... | collective-permute-start | bytes 393224 | tf_op jit(solution)/shard_map/while/body/eval_jaxpr/ppermute | solution.py:12
  169.6 8.1 %collective-permute-start = (bf16[32,2048]{1,0:T(8,128)(2,1)S(1)}, bf16[32,2048]{1,0:T(8,128)(2,1)S(1)}, u32[]{:S(2)}, u32[]{:S(2)}) collective-permute-start(bf16[32,2048]{1,0:T(8,128)(2,1)S(1)} %get-tuple-element.350), channel_id=1, source_target_pairs={{248,0},{0,8},{8,16},{16,24},{24,32},{32,40},{40,48},{48,56},{56,6... | collective-permute-start | bytes 393224 | tf_op jit(solution)/shard_map/while/body/eval_jaxpr/ppermute | solution.py:12
  180.9 8.1 %collective-permute-start = (bf16[32,2048]{1,0:T(8,128)(2,1)S(1)}, bf16[32,2048]{1,0:T(8,128)(2,1)S(1)}, u32[]{:S(2)}, u32[]{:S(2)}) collective-permute-start(bf16[32,2048]{1,0:T(8,128)(2,1)S(1)} %get-tuple-element.350), channel_id=1, source_target_pairs={{248,0},{0,8},{8,16},{16,24},{24,32},{32,40},{40,48},{48,56},{56,6... | collective-permute-start | bytes 393224 | tf_op jit(solution)/shard_map/while/body/eval_jaxpr/ppermute | solution.py:12
  192.3 8.1 %collective-permute-start = (bf16[32,2048]{1,0:T(8,128)(2,1)S(1)}, bf16[32,2048]{1,0:T(8,128)(2,1)S(1)}, u32[]{:S(2)}, u32[]{:S(2)}) collective-permute-start(bf16[32,2048]{1,0:T(8,128)(2,1)S(1)} %get-tuple-element.350), channel_id=1, source_target_pairs={{248,0},{0,8},{8,16},{16,24},{24,32},{32,40},{40,48},{48,56},{56,6... | collective-permute-start | bytes 393224 | tf_op jit(solution)/shard_map/while/body/eval_jaxpr/ppermute | solution.py:12
  203.7 8.1 %collective-permute-start = (bf16[32,2048]{1,0:T(8,128)(2,1)S(1)}, bf16[32,2048]{1,0:T(8,128)(2,1)S(1)}, u32[]{:S(2)}, u32[]{:S(2)}) collective-permute-start(bf16[32,2048]{1,0:T(8,128)(2,1)S(1)} %get-tuple-element.350), channel_id=1, source_target_pairs={{248,0},{0,8},{8,16},{16,24},{24,32},{32,40},{40,48},{48,56},{56,6... | collective-permute-start | bytes 393224 | tf_op jit(solution)/shard_map/while/body/eval_jaxpr/ppermute | solution.py:12
  215.2 8.1 %collective-permute-start = (bf16[32,2048]{1,0:T(8,128)(2,1)S(1)}, bf16[32,2048]{1,0:T(8,128)(2,1)S(1)}, u32[]{:S(2)}, u32[]{:S(2)}) collective-permute-start(bf16[32,2048]{1,0:T(8,128)(2,1)S(1)} %get-tuple-element.350), channel_id=1, source_target_pairs={{248,0},{0,8},{8,16},{16,24},{24,32},{32,40},{40,48},{48,56},{56,6... | collective-permute-start | bytes 393224 | tf_op jit(solution)/shard_map/while/body/eval_jaxpr/ppermute | solution.py:12
  226.6 8.1 %collective-permute-start = (bf16[32,2048]{1,0:T(8,128)(2,1)S(1)}, bf16[32,2048]{1,0:T(8,128)(2,1)S(1)}, u32[]{:S(2)}, u32[]{:S(2)}) collective-permute-start(bf16[32,2048]{1,0:T(8,128)(2,1)S(1)} %get-tuple-element.350), channel_id=1, source_target_pairs={{248,0},{0,8},{8,16},{16,24},{24,32},{32,40},{40,48},{48,56},{56,6... | collective-permute-start | bytes 393224 | tf_op jit(solution)/shard_map/while/body/eval_jaxpr/ppermute | solution.py:12
  238.0 8.1 %collective-permute-start = (bf16[32,2048]{1,0:T(8,128)(2,1)S(1)}, bf16[32,2048]{1,0:T(8,128)(2,1)S(1)}, u32[]{:S(2)}, u32[]{:S(2)}) collective-permute-start(bf16[32,2048]{1,0:T(8,128)(2,1)S(1)} %get-tuple-element.350), channel_id=1, source_target_pairs={{248,0},{0,8},{8,16},{16,24},{24,32},{32,40},{40,48},{48,56},{56,6... | collective-permute-start | bytes 393224 | tf_op jit(solution)/shard_map/while/body/eval_jaxpr/ppermute | solution.py:12
  249.4 8.1 %collective-permute-start = (bf16[32,2048]{1,0:T(8,128)(2,1)S(1)}, bf16[32,2048]{1,0:T(8,128)(2,1)S(1)}, u32[]{:S(2)}, u32[]{:S(2)}) collective-permute-start(bf16[32,2048]{1,0:T(8,128)(2,1)S(1)} %get-tuple-element.350), channel_id=1, source_target_pairs={{248,0},{0,8},{8,16},{16,24},{24,32},{32,40},{40,48},{48,56},{56,6... | collective-permute-start | bytes 393224 | tf_op jit(solution)/shard_map/while/body/eval_jaxpr/ppermute | solution.py:12
  260.8 8.1 %collective-permute-start = (bf16[32,2048]{1,0:T(8,128)(2,1)S(1)}, bf16[32,2048]{1,0:T(8,128)(2,1)S(1)}, u32[]{:S(2)}, u32[]{:S(2)}) collective-permute-start(bf16[32,2048]{1,0:T(8,128)(2,1)S(1)} %get-tuple-element.350), channel_id=1, source_target_pairs={{248,0},{0,8},{8,16},{16,24},{24,32},{32,40},{40,48},{48,56},{56,6... | collective-permute-start | bytes 393224 | tf_op jit(solution)/shard_map/while/body/eval_jaxpr/ppermute | solution.py:12
  272.2 8.1 %collective-permute-start = (bf16[32,2048]{1,0:T(8,128)(2,1)S(1)}, bf16[32,2048]{1,0:T(8,128)(2,1)S(1)}, u32[]{:S(2)}, u32[]{:S(2)}) collective-permute-start(bf16[32,2048]{1,0:T(8,128)(2,1)S(1)} %get-tuple-element.350), channel_id=1, source_target_pairs={{248,0},{0,8},{8,16},{16,24},{24,32},{32,40},{40,48},{48,56},{56,6... | collective-permute-start | bytes 393224 | tf_op jit(solution)/shard_map/while/body/eval_jaxpr/ppermute | solution.py:12
  283.6 8.1 %collective-permute-start = (bf16[32,2048]{1,0:T(8,128)(2,1)S(1)}, bf16[32,2048]{1,0:T(8,128)(2,1)S(1)}, u32[]{:S(2)}, u32[]{:S(2)}) collective-permute-start(bf16[32,2048]{1,0:T(8,128)(2,1)S(1)} %get-tuple-element.350), channel_id=1, source_target_pairs={{248,0},{0,8},{8,16},{16,24},{24,32},{32,40},{40,48},{48,56},{56,6... | collective-permute-start | bytes 393224 | tf_op jit(solution)/shard_map/while/body/eval_jaxpr/ppermute | solution.py:12
  295.0 8.1 %collective-permute-start = (bf16[32,2048]{1,0:T(8,128)(2,1)S(1)}, bf16[32,2048]{1,0:T(8,128)(2,1)S(1)}, u32[]{:S(2)}, u32[]{:S(2)}) collective-permute-start(bf16[32,2048]{1,0:T(8,128)(2,1)S(1)} %get-tuple-element.350), channel_id=1, source_target_pairs={{248,0},{0,8},{8,16},{16,24},{24,32},{32,40},{40,48},{48,56},{56,6... | collective-permute-start | bytes 393224 | tf_op jit(solution)/shard_map/while/body/eval_jaxpr/ppermute | solution.py:12
  306.4 8.1 %collective-permute-start = (bf16[32,2048]{1,0:T(8,128)(2,1)S(1)}, bf16[32,2048]{1,0:T(8,128)(2,1)S(1)}, u32[]{:S(2)}, u32[]{:S(2)}) collective-permute-start(bf16[32,2048]{1,0:T(8,128)(2,1)S(1)} %get-tuple-element.350), channel_id=1, source_target_pairs={{248,0},{0,8},{8,16},{16,24},{24,32},{32,40},{40,48},{48,56},{56,6... | collective-permute-start | bytes 393224 | tf_op jit(solution)/shard_map/while/body/eval_jaxpr/ppermute | solution.py:12
  317.8 8.1 %collective-permute-start = (bf16[32,2048]{1,0:T(8,128)(2,1)S(1)}, bf16[32,2048]{1,0:T(8,128)(2,1)S(1)}, u32[]{:S(2)}, u32[]{:S(2)}) collective-permute-start(bf16[32,2048]{1,0:T(8,128)(2,1)S(1)} %get-tuple-element.350), channel_id=1, source_target_pairs={{248,0},{0,8},{8,16},{16,24},{24,32},{32,40},{40,48},{48,56},{56,6... | collective-permute-start | bytes 393224 | tf_op jit(solution)/shard_map/while/body/eval_jaxpr/ppermute | solution.py:12
  329.2 8.1 %collective-permute-start = (bf16[32,2048]{1,0:T(8,128)(2,1)S(1)}, bf16[32,2048]{1,0:T(8,128)(2,1)S(1)}, u32[]{:S(2)}, u32[]{:S(2)}) collective-permute-start(bf16[32,2048]{1,0:T(8,128)(2,1)S(1)} %get-tuple-element.350), channel_id=1, source_target_pairs={{248,0},{0,8},{8,16},{16,24},{24,32},{32,40},{40,48},{48,56},{56,6... | collective-permute-start | bytes 393224 | tf_op jit(solution)/shard_map/while/body/eval_jaxpr/ppermute | solution.py:12
  340.6 8.1 %collective-permute-start = (bf16[32,2048]{1,0:T(8,128)(2,1)S(1)}, bf16[32,2048]{1,0:T(8,128)(2,1)S(1)}, u32[]{:S(2)}, u32[]{:S(2)}) collective-permute-start(bf16[32,2048]{1,0:T(8,128)(2,1)S(1)} %get-tuple-element.350), channel_id=1, source_target_pairs={{248,0},{0,8},{8,16},{16,24},{24,32},{32,40},{40,48},{48,56},{56,6... | collective-permute-start | bytes 393224 | tf_op jit(solution)/shard_map/while/body/eval_jaxpr/ppermute | solution.py:12
  352.0 8.2 %collective-permute-start = (bf16[32,2048]{1,0:T(8,128)(2,1)S(1)}, bf16[32,2048]{1,0:T(8,128)(2,1)S(1)}, u32[]{:S(2)}, u32[]{:S(2)}) collective-permute-start(bf16[32,2048]{1,0:T(8,128)(2,1)S(1)} %get-tuple-element.350), channel_id=1, source_target_pairs={{248,0},{0,8},{8,16},{16,24},{24,32},{32,40},{40,48},{48,56},{56,6... | collective-permute-start | bytes 393224 | tf_op jit(solution)/shard_map/while/body/eval_jaxpr/ppermute | solution.py:12
  364.7 16.0 %all-to-all-start = ((bf16[8,32,2048]{2,1,0:T(8,128)(2,1)}), bf16[8,32,2048]{2,1,0:T(8,128)(2,1)S(1)}, u32[]{:S(2)}, u32[]{:S(2)}) async-start(bf16[8,32,2048]{2,1,0:T(8,128)(2,1)} %stack.2), calls=%async_computation | async-start | bytes 2097152 | tf_op jit(solution)/shard_map/all_to_all | solution.py:64
